TPU v7x, 32 devices: a whole 2x2x4 slice. The times are simulated.
32 devices in a mesh: groups: 2 (over y), dp: 4 (over z), feat: 2 (over core), ens: 2 (over x).
Axes of the slice: x: 2, y: 2, z: 4, core: 2. Of those that a mesh axis runs over, the one named last changes fastest.
Arguments:
- test_feat: bfloat16 [2, 64, 8192], P('ens', 'groups', 'dp'), parts along dimension 1, may hold values from -6 to 6
- kernel_inverse: bfloat16 [2, 8192, 8192], P('ens', 'dp', 'feat'), may hold values from -0.0625 to 0.0625
- train_feat: bfloat16 [2, 1024, 8192], P('ens', 'dp', 'feat'), may hold values from -0.0625 to 0.0625
- residual_weight: float32 [2, 1024], P('ens', 'dp'), may hold values from 0.05 to 1
Outputs:
- scores: float32 [64, 1024], P(('groups', 'feat', 'ens'), 'dp'), parts along dimension 0
There are 2 independent parts, one for each index of `groups`. A program takes and returns all parts, laid end to end along the dimension named above; an argument that names none is the same for every part. Nothing has to cross between parts.
All inputs are finite; a program needn't handle non-finite values.
Results may differ from a plain program's by a relative error of at most 0.0029.
Values may be sent and summed in bfloat16 or wider, within the bound.
A program may use at most 64 MiB of HBM per device.

v0:
```python
import jax
import jax.numpy as jnp
from jax import lax
from jax.sharding import PartitionSpec as P


def shards(test_feat, kernel_inverse, train_feat, residual_weight):
    test_local = test_feat[0]
    inverse_local = kernel_inverse[0]
    train_local = train_feat[0]
    weight_row = residual_weight[0][None, :]
    partial_sum = jnp.dot(test_local, inverse_local, preferred_element_type=jnp.float32)
    projected = lax.psum(partial_sum, "dp").astype(jnp.bfloat16)
    raw = jnp.einsum("tf,nf->tn", projected, train_local, preferred_element_type=jnp.float32)
    totals = raw * weight_row
    return lax.psum_scatter(totals, ("feat", "ens"), scatter_dimension=0, tiled=True)


def solution(mesh):
    in_specs = (
        P("ens", "groups", "dp"),
        P("ens", "dp", "feat"),
        P("ens", "dp", "feat"),
        P("ens", "dp"),
    )
    out_specs = P(("groups", "feat", "ens"), "dp")
    return jax.shard_map(shards, mesh=mesh, in_specs=in_specs, out_specs=out_specs, check_vma=False)
```

profile of v0, /device:TPU:0, one launch (start us, length us, event | category | flops | bytes accessed | tf_op | source)
XLA Modules:
  0.0 74.1 jit_solution(5447746823196072305)
XLA Ops:
  6.5 0.0 copy-start
  6.5 0.0 copy-start.1
  6.5 0.0 reduce-scatter.2.cloned.1.call-start
  6.5 9.0 %fusion = f32[32,4096]{1,0:T(8,128)S(1)} fusion(bf16[1,2048,4096]{2,1,0:T(8,128)(2,1)} %param.5, bf16[1,32,2048]{2,1,0:T(8,128)(2,1)} %param.4), kind=kOutput, calls=%fused_computation | convolution fusion | flops 536870912 | bytes 17432576 | tf_op jit(solution)/shard_map/dot_general | solution.py:12
  15.5 32.1 %all-reduce.1 = bf16[32,4096]{1,0:T(8,128)(2,1)S(1)} all-reduce(f32[32,4096]{1,0:T(8,128)S(1)} %fusion), channel_id=1, replica_groups=mesh['groups'=2,'dp'=4,'feat'=2,'ens'=2] {'dp'}, use_global_device_ids=true, to_apply=%region_0.0 | all-reduce | flops 131072 | bytes 786432 | tf_op jit(solution)/shard_map/psum | solution.py:13
  47.6 0.0 copy-done
  47.6 0.0 copy-done.1
  47.6 1.3 %fusion.4 = f32[32,256]{1,0:T(8,128)} fusion(bf16[1,256,4096]{2,1,0:T(8,128)(2,1)S(1)} %copy-done, bf16[32,4096]{1,0:T(8,128)(2,1)S(1)} %all-reduce.1, f32[256]{0:T(256)S(1)} %bitcast.13), kind=kOutput, calls=%fused_computation.4 | convolution fusion | flops 67117056 | bytes 2393088 | tf_op jit(solution)/shard_map/tf,nf->tn/dot_general | solution.py:14
  49.0 0.0 reduce-scatter.2.cloned.1.call-update
  49.0 18.2 %reduce-scatter.2.cloned.1.call-done = f32[8,256]{1,0:T(8,128)} async-done(((f32[32,256]{1,0:T(8,128)}), f32[8,256]{1,0:T(8,128)}) %reduce-scatter.2.cloned.1.call-update) | async-done | bytes 8208 | tf_op jit(solution)/shard_map/reduce_scatter | solution.py:16
Async XLA Ops:
  6.5 41.1 %copy-start = (bf16[1,256,4096]{2,1,0:T(8,128)(2,1)S(1)}, bf16[1,256,4096]{2,1,0:T(8,128)(2,1)}, u32[]{:S(2)}) copy-start(bf16[1,256,4096]{2,1,0:T(8,128)(2,1)} %param.6) | copy-start | bytes 6291460
  6.5 41.1 %copy-start.1 = (f32[1,256]{1,0:T(1,128)S(1)}, f32[1,256]{1,0:T(1,128)}, u32[]{:S(2)}) copy-start(f32[1,256]{1,0:T(1,128)} %param.7) | copy-start | bytes 3076
  6.5 60.7 %reduce-scatter.2.cloned.1.call-start = ((), (), s32[]{:S(2)}) async-start(), calls=%async_computation.1 | async-start | bytes 40960 | tf_op jit(solution)/shard_map/reduce_scatter | solution.py:16
Sparse Core Ops, SparseCore 0:
  49.1 18.0 reduce-scatter.1
where the time goes:
time: 74.3 us; the launch traced here: 74.1 us
  blocking collectives  32.1 us (43%)
  waiting for transfers between devices  18.3 us (25%)
  between operations  13.4 us (18%)
  matrix products  10.3 us (14%)
    psum x1, blocking collectives, shards(): projected = lax.psum(partial_sum, 'dp').astype(jnp.bfloat16)  32.1 us
    reduce_scatter x1, waiting for transfers between devices, shards(): lax.psum_scatter(totals, ('feat', 'ens'), scatter_dimension=0, tiled=True)  18.2 us
    dot_general x1, matrix products, shards(): jnp.dot(test_local, inverse_local, preferred_element_type=jnp.float32)  8.96 us
  transfers between devices with their start and end apart: 1, of which 1 were waited for; matrix products, arithmetic and copies ran while one was open for 0% of the time, Pallas kernels for 0%

commit v1 on v0

v1 whole, which is shorter than its diff:
```python
import functools

import jax
import jax.numpy as jnp
from jax import lax
from jax.experimental import pallas as pl
from jax.experimental.pallas import tpu as pltpu
from jax.sharding import PartitionSpec as P

MESH = pl.DeviceIdType.MESH


def kernel(n, feats, models, rounds, test_hbm, inv_hbm, train_hbm, weight_ref, out_ref,
           test_v, inv_v, train_v, part_f, part_b, got, proj, totals, pieces,
           load_sem, inv_sem, rs_send, rs_recv, ag_send, ag_recv, fin_send, fin_recv):
    me = lax.axis_index("dp")
    my_feat, my_model = lax.axis_index("feat"), lax.axis_index("ens")
    rows, depth = test_v.shape
    wide = inv_v.shape[2]
    chunk = wide // n
    finals = feats * models
    spot = my_feat * models + my_model
    each = rows // finals

    test_load = pltpu.make_async_copy(test_hbm.at[0], test_v, load_sem.at[0])
    test_load.start()
    inv_loads = []
    for r in range(rounds):
        load = pltpu.make_async_copy(inv_hbm.at[0, :, pl.ds(r * wide, wide)], inv_v.at[r], inv_sem.at[r])
        load.start()
        inv_loads.append(load)
    train_load = pltpu.make_async_copy(train_hbm.at[0], train_v, load_sem.at[1])
    train_load.start()

    barrier = pltpu.get_barrier_semaphore()
    for k in range(1, n):
        pl.semaphore_signal(barrier, inc=1, device_id={"dp": lax.rem(me + k, n)}, device_id_type=MESH)

    def other(k):
        target = lax.rem(spot + k, finals)
        return target, {"feat": target // models, "ens": lax.rem(target, models)}

    for k in range(1, finals):
        pl.semaphore_signal(barrier, inc=1, device_id=other(k)[1], device_id_type=MESH)
    pl.semaphore_wait(barrier, n - 1 + finals - 1)

    test_load.wait()
    scatters = {}
    gathers = {}

    def project(r):
        inv_loads[r].wait()
        term = jnp.dot(test_v[...], inv_v[r], preferred_element_type=jnp.float32)
        for d in range(n):
            piece = term[:, d * chunk:(d + 1) * chunk]
            part_f[r, d] = piece
            part_b[r, d] = piece.astype(jnp.bfloat16)
        scatters[r] = []
        for k in range(1, n):
            target = lax.rem(me + k, n)
            copy = pltpu.make_async_remote_copy(
                src_ref=part_b.at[r, target], dst_ref=got.at[r, k - 1],
                send_sem=rs_send.at[r, k - 1], recv_sem=rs_recv.at[r, k - 1],
                device_id={"dp": target}, device_id_type=MESH)
            copy.start()
            scatters[r].append(copy)

    def gather(r):
        total = part_f[r, me]
        for k in range(1, n):
            scatters[r][k - 1].wait_recv()
            total = total + got[r, k - 1].astype(jnp.float32)
        proj[r, me] = total.astype(jnp.bfloat16)
        gathers[r] = []
        for k in range(1, n):
            copy = pltpu.make_async_remote_copy(
                src_ref=proj.at[r, me], dst_ref=proj.at[r, me],
                send_sem=ag_send.at[r, k - 1], recv_sem=ag_recv.at[r, k - 1],
                device_id={"dp": lax.rem(me + k, n)}, device_id_type=MESH)
            copy.start()
            gathers[r].append(copy)

    def score(r, raw):
        for copy in gathers[r]:
            copy.wait_recv()
        for d in range(n):
            at = r * wide + d * chunk
            raw = raw + lax.dot_general(
                proj[r, d], train_v[:, at:at + chunk], (((1,), (1,)), ((), ())),
                preferred_element_type=jnp.float32)
        return raw

    raw = jnp.zeros((rows, train_v.shape[0]), jnp.float32)
    for r in range(rounds):
        project(r)
        if r >= 1:
            gather(r - 1)
    gather(rounds - 1)
    train_load.wait()
    for r in range(rounds):
        raw = score(r, raw)

    weighted = raw * weight_ref[...]
    for j in range(finals):
        totals[j] = weighted[j * each:(j + 1) * each]
    last = []
    for k in range(1, finals):
        target, where = other(k)
        copy = pltpu.make_async_remote_copy(
            src_ref=totals.at[target], dst_ref=pieces.at[k - 1],
            send_sem=fin_send.at[k - 1], recv_sem=fin_recv.at[k - 1],
            device_id=where, device_id_type=MESH)
        copy.start()
        last.append(copy)
    done = totals[spot]
    for k in range(1, finals):
        last[k - 1].wait_recv()
        done = done + pieces[k - 1]
    out_ref[...] = done
    for r in range(rounds):
        for copy in scatters[r] + gathers[r]:
            copy.wait_send()
    for copy in last:
        copy.wait_send()


def solution(mesh):
    n, feats, models = mesh.shape["dp"], mesh.shape["feat"], mesh.shape["ens"]
    finals = feats * models

    def shards(test_feat, kernel_inverse, train_feat, residual_weight):
        _, rows, depth = test_feat.shape
        width = kernel_inverse.shape[2]
        cols = train_feat.shape[1]
        rounds = max(1, min(4, width // (n * 256)))
        wide = width // rounds
        chunk = wide // n
        bf16, f32 = jnp.bfloat16, jnp.float32
        any_space = pl.BlockSpec(memory_space=pl.ANY)
        in_vmem = pl.BlockSpec(memory_space=pltpu.VMEM)
        dma = pltpu.SemaphoreType.DMA
        return pl.pallas_call(
            functools.partial(kernel, n, feats, models, rounds),
            out_shape=jax.ShapeDtypeStruct((rows // finals, cols), f32),
            in_specs=[any_space, any_space, any_space, in_vmem],
            out_specs=in_vmem,
            scratch_shapes=[
                pltpu.VMEM((rows, depth), bf16),
                pltpu.VMEM((rounds, depth, wide), bf16),
                pltpu.VMEM((cols, width), bf16),
                pltpu.VMEM((rounds, n, rows, chunk), f32),
                pltpu.VMEM((rounds, n, rows, chunk), bf16),
                pltpu.VMEM((rounds, n - 1, rows, chunk), bf16),
                pltpu.VMEM((rounds, n, rows, chunk), bf16),
                pltpu.VMEM((finals, rows // finals, cols), f32),
                pltpu.VMEM((finals - 1, rows // finals, cols), f32),
                dma((2,)), dma((rounds,)),
                dma((rounds, n - 1)), dma((rounds, n - 1)),
                dma((rounds, n - 1)), dma((rounds, n - 1)),
                dma((finals - 1,)), dma((finals - 1,)),
            ],
            compiler_params=pltpu.CompilerParams(
                collective_id=0, has_side_effects=True, vmem_limit_bytes=60 * 1024 * 1024),
        )(test_feat, kernel_inverse, train_feat, residual_weight)

    in_specs = (
        P("ens", "groups", "dp"),
        P("ens", "dp", "feat"),
        P("ens", "dp", "feat"),
        P("ens", "dp"),
    )
    out_specs = P(("groups", "feat", "ens"), "dp")
    return jax.shard_map(shards, mesh=mesh, in_specs=in_specs, out_specs=out_specs, check_vma=False)
```

time: 74.3 us -> 30.2 us (0.41)
  blocking collectives: 32.1 us -> 0 us
  Pallas kernels: 0 us -> 28.7 us
  waiting for transfers between devices: 18.3 us -> 0 us
  between operations: 13.4 us -> 0.01 us
  matrix products: 10.3 us -> 0 us
  local copies, waits for them, and re-layouts: 0.01 us -> 1.3 us
    psum x1 -> x0, blocking collectives: 32.1 us -> none  [shards(): projected = lax.psum(partial_sum, 'dp').astype(jnp.bfloat16)]
    pallas_call x0 -> x1, Pallas kernels: none -> 28.7 us  [shards(): pl.pallas_call(functools.partial(kernel, n, feats, models, rounds), out_s...]
    reduce_scatter x1 -> x0, waiting for transfers between devices: 18.2 us -> none  [shards(): lax.psum_scatter(totals, ('feat', 'ens'), scatter_dimension=0, tiled=True)]
    dot_general x2 -> x0, matrix products: 10.3 us -> none  [the longest x1 8.96 us: shards(): jnp.dot(test_local, inverse_local, preferred_element_type=jnp.float32)]
    unnamed x4 -> x1, local copies, waits for them, and re-layouts: 0.01 us -> 1.3 us
  transfers between devices with their start and end apart: 1 -> 0, of which waited for: 1 -> 0; matrix products, arithmetic and copies ran while one was open for 0% -> 0% of each run, Pallas kernels for 0% -> 0%
where the time goes in v1:
time: 30.2 us; the launch traced here: 30 us
  Pallas kernels  28.7 us (95%)
  local copies, waits for them, and re-layouts  1.3 us (4%)
    pallas_call x1, Pallas kernels, shards(): pl.pallas_call(functools.partial(kernel, n, feats, models, rounds), out_s...  28.7 us
    unnamed x1, local copies, waits for them, and re-layouts  1.3 us

profile of v1, /device:TPU:0, one launch (start us, length us, event | category | flops | bytes accessed | tf_op | source)
XLA Modules:
  0.0 30.0 jit_solution(5739990232666372771)
XLA Ops:
  0.0 28.7 %shard_map.46 = f32[8,256]{1,0:T(8,128)} custom-call(bf16[1,32,2048]{2,1,0:T(8,128)(2,1)} %test_hbm.1, bf16[1,2048,4096]{2,1,0:T(8,128)(2,1)} %inv_hbm.1, bf16[1,256,4096]{2,1,0:T(8,128)(2,1)} %train_hbm.1, f32[1,256]{1,0:T(1,128)} %weight_ref.1), custom_call_target="tpu_custom_call" | custom-call | tf_op jit(solution)/shard_map/pallas_call | solution.py:142
  28.7 1.3 %copy.6 = f32[8,256]{1,0:T(8,128)} copy(f32[8,256]{1,0:T(8,128)} %shard_map.46) | data formatting | bytes 16384

commit v2 on v1

v2 whole, which is shorter than its diff:
```python
import functools

import jax
import jax.numpy as jnp
from jax import lax
from jax.experimental import pallas as pl
from jax.experimental.pallas import tpu as pltpu
from jax.sharding import PartitionSpec as P

MESH = pl.DeviceIdType.MESH


def kernel(n, feats, models, rounds, test_hbm, inv_hbm, train_hbm, weight_ref, out_ref,
           test_v, inv_v, train_v, own, carried, from_outer, from_middle, proj, raw, totals, pieces,
           load_sem, inv_sem, in_send, outer_recv, middle_recv, out_send, out_recv, fin_send, fin_recv):
    me = lax.axis_index("dp")
    my_feat, my_model = lax.axis_index("feat"), lax.axis_index("ens")
    rows = test_v.shape[0]
    wide = inv_v.shape[2]
    finals = feats * models
    spot = my_feat * models + my_model
    each = rows // finals
    half = n // 2
    low = me < half
    inward = jnp.where(low, me + 1, me - 1)
    outward = jnp.where(low, jnp.maximum(me - 1, 0), jnp.minimum(me + 1, n - 1))
    height = jnp.where(low, me, n - 1 - me)
    has_outer = height > 0
    middle = height == half - 1
    lag = 3

    def other(k):
        target = lax.rem(spot + k, finals)
        return target, {"feat": target // models, "ens": lax.rem(target, models)}

    test_load = pltpu.make_async_copy(test_hbm.at[0], test_v, load_sem.at[0])
    test_load.start()
    inv_loads = []
    for r in range(rounds):
        load = pltpu.make_async_copy(inv_hbm.at[0, :, pl.ds(r * wide, wide)], inv_v.at[r], inv_sem.at[r])
        load.start()
        inv_loads.append(load)
    train_load = pltpu.make_async_copy(train_hbm.at[0], train_v, load_sem.at[1])
    train_load.start()

    barrier = pltpu.get_barrier_semaphore()
    pl.semaphore_signal(barrier, inc=1, device_id={"dp": inward}, device_id_type=MESH)

    @pl.when(has_outer)
    def _():
        pl.semaphore_signal(barrier, inc=1, device_id={"dp": outward}, device_id_type=MESH)

    for k in range(1, finals):
        pl.semaphore_signal(barrier, inc=1, device_id=other(k)[1], device_id_type=MESH)
    raw[...] = jnp.zeros_like(raw)
    test_load.wait()
    pl.semaphore_wait(barrier, jnp.where(has_outer, finals + 1, finals))

    def to_next(r):
        return pltpu.make_async_remote_copy(
            src_ref=carried.at[r], dst_ref=from_outer.at[r], send_sem=in_send.at[r],
            recv_sem=outer_recv.at[r], device_id={"dp": inward}, device_id_type=MESH)

    def to_middle(r):
        return pltpu.make_async_remote_copy(
            src_ref=carried.at[r], dst_ref=from_middle.at[r], send_sem=in_send.at[r],
            recv_sem=middle_recv.at[r], device_id={"dp": inward}, device_id_type=MESH)

    def to_outer(r):
        return pltpu.make_async_remote_copy(
            src_ref=proj.at[r], dst_ref=proj.at[r], send_sem=out_send.at[r],
            recv_sem=out_recv.at[r], device_id={"dp": outward}, device_id_type=MESH)

    def project(r):
        inv_loads[r].wait()
        own[r] = jnp.dot(test_v[...], inv_v[r], preferred_element_type=jnp.float32)

    def add_outer(r):
        @pl.when(has_outer)
        def _():
            to_next(r).wait_recv()
            own[r] += from_outer[r].astype(jnp.float32)
        carried[r] = own[r].astype(carried.dtype)

    def pass_out(r):
        @pl.when(has_outer)
        def _():
            to_outer(r).start()

    def score(r):
        raw[...] += lax.dot_general(
            proj[r], train_v[:, r * wide:(r + 1) * wide], (((1,), (1,)), ((), ())),
            preferred_element_type=jnp.float32)

    @pl.when(middle)
    def _():
        def finish(r):
            to_middle(r).wait_recv()
            proj[r] = (own[r] + from_middle[r].astype(jnp.float32)).astype(proj.dtype)
            pass_out(r)
            if r == 0:
                train_load.wait()
            score(r)

        for r in range(rounds):
            project(r)
            add_outer(r)
            to_middle(r).start()
            if r >= lag:
                finish(r - lag)
        for r in range(max(rounds - lag, 0), rounds):
            finish(r)
        for r in range(rounds):
            to_middle(r).wait_send()

    @pl.when(jnp.logical_not(middle))
    def _():
        for r in range(rounds):
            project(r)
            add_outer(r)
            to_next(r).start()
        train_load.wait()
        for r in range(rounds):
            to_outer(r).wait_recv()
            pass_out(r)
            score(r)
        for r in range(rounds):
            to_next(r).wait_send()

    weighted = raw[...] * weight_ref[...]
    for j in range(finals):
        totals[j] = weighted[j * each:(j + 1) * each]
    last = []
    for k in range(1, finals):
        target, where = other(k)
        copy = pltpu.make_async_remote_copy(
            src_ref=totals.at[target], dst_ref=pieces.at[k - 1],
            send_sem=fin_send.at[k - 1], recv_sem=fin_recv.at[k - 1],
            device_id=where, device_id_type=MESH)
        copy.start()
        last.append(copy)
    done = totals[spot]
    for k in range(1, finals):
        last[k - 1].wait_recv()
        done = done + pieces[k - 1]
    out_ref[...] = done

    @pl.when(has_outer)
    def _():
        for r in range(rounds):
            to_outer(r).wait_send()

    for copy in last:
        copy.wait_send()


def solution(mesh):
    n, feats, models = mesh.shape["dp"], mesh.shape["feat"], mesh.shape["ens"]
    finals = feats * models

    def shards(test_feat, kernel_inverse, train_feat, residual_weight):
        _, rows, depth = test_feat.shape
        width = kernel_inverse.shape[2]
        cols = train_feat.shape[1]
        rounds = max(1, min(8, width // 512))
        wide = width // rounds
        bf16, f32 = jnp.bfloat16, jnp.float32
        carry = bf16 if n <= 4 else f32
        any_space = pl.BlockSpec(memory_space=pl.ANY)
        in_vmem = pl.BlockSpec(memory_space=pltpu.VMEM)
        dma = pltpu.SemaphoreType.DMA
        return pl.pallas_call(
            functools.partial(kernel, n, feats, models, rounds),
            out_shape=jax.ShapeDtypeStruct((rows // finals, cols), f32),
            in_specs=[any_space, any_space, any_space, in_vmem],
            out_specs=in_vmem,
            scratch_shapes=[
                pltpu.VMEM((rows, depth), bf16),
                pltpu.VMEM((rounds, depth, wide), bf16),
                pltpu.VMEM((cols, width), bf16),
                pltpu.VMEM((rounds, rows, wide), f32),
                pltpu.VMEM((rounds, rows, wide), carry),
                pltpu.VMEM((rounds, rows, wide), carry),
                pltpu.VMEM((rounds, rows, wide), carry),
                pltpu.VMEM((rounds, rows, wide), bf16),
                pltpu.VMEM((rows, cols), f32),
                pltpu.VMEM((finals, rows // finals, cols), f32),
                pltpu.VMEM((finals - 1, rows // finals, cols), f32),
                dma((2,)), dma((rounds,)),
                dma((rounds,)), dma((rounds,)), dma((rounds,)), dma((rounds,)), dma((rounds,)),
                dma((finals - 1,)), dma((finals - 1,)),
            ],
            compiler_params=pltpu.CompilerParams(
                collective_id=0, has_side_effects=True, vmem_limit_bytes=60 * 1024 * 1024),
        )(test_feat, kernel_inverse, train_feat, residual_weight)

    in_specs = (
        P("ens", "groups", "dp"),
        P("ens", "dp", "feat"),
        P("ens", "dp", "feat"),
        P("ens", "dp"),
    )
    out_specs = P(("groups", "feat", "ens"), "dp")
    return jax.shard_map(shards, mesh=mesh, in_specs=in_specs, out_specs=out_specs, check_vma=False)
```

time: 30.2 us -> 29.1 us (0.964)
  Pallas kernels: 28.7 us -> 27.6 us
    pallas_call x1, Pallas kernels: 28.7 us -> 27.6 us  [shards(): pl.pallas_call(functools.partial(kernel, n, feats, models, rounds), out_s...]
where the time goes in v2:
time: 29.1 us; the launch traced here: 28.9 us
  Pallas kernels  27.6 us (95%)
  local copies, waits for them, and re-layouts  1.3 us (4%)
    pallas_call x1, Pallas kernels, shards(): pl.pallas_call(functools.partial(kernel, n, feats, models, rounds), out_s...  27.6 us
    unnamed x1, local copies, waits for them, and re-layouts  1.3 us

profile of v2, /device:TPU:0, one launch (start us, length us, event | category | flops | bytes accessed | tf_op | source)
XLA Modules:
  0.0 28.9 jit_solution(10043507323009549902)
XLA Ops:
  0.0 27.6 %shard_map.46 = f32[8,256]{1,0:T(8,128)} custom-call(bf16[1,32,2048]{2,1,0:T(8,128)(2,1)} %test_hbm.1, bf16[1,2048,4096]{2,1,0:T(8,128)(2,1)} %inv_hbm.1, bf16[1,256,4096]{2,1,0:T(8,128)(2,1)} %train_hbm.1, f32[1,256]{1,0:T(1,128)} %weight_ref.1), custom_call_target="tpu_custom_call" | custom-call | tf_op jit(solution)/shard_map/pallas_call | solution.py:172
  27.6 1.3 %copy.6 = f32[8,256]{1,0:T(8,128)} copy(f32[8,256]{1,0:T(8,128)} %shard_map.46) | data formatting | bytes 16384

commit v3 on v2

--- a/solution.py
+++ b/solution.py
@@ -27,7 +27,7 @@
     height = jnp.where(low, me, n - 1 - me)
     has_outer = height > 0
     middle = height == half - 1
-    lag = 3
+    lag = 4
 
     def other(k):
         target = lax.rem(spot + k, finals)
@@ -162,7 +162,7 @@
         _, rows, depth = test_feat.shape
         width = kernel_inverse.shape[2]
         cols = train_feat.shape[1]
-        rounds = max(1, min(8, width // 512))
+        rounds = max(1, min(4, width // 512))
         wide = width // rounds
         bf16, f32 = jnp.bfloat16, jnp.float32
         carry = bf16 if n <= 4 else f32

time: 29.1 us -> 28.2 us (0.969)
  Pallas kernels: 27.6 us -> 26.7 us
    pallas_call x1, Pallas kernels: 27.6 us -> 26.7 us  [shards(): pl.pallas_call(functools.partial(kernel, n, feats, models, rounds), out_s...]
where the time goes in v3:
time: 28.2 us; the launch traced here: 28 us
  Pallas kernels  26.7 us (95%)
  local copies, waits for them, and re-layouts  1.3 us (5%)
    pallas_call x1, Pallas kernels, shards(): pl.pallas_call(functools.partial(kernel, n, feats, models, rounds), out_s...  26.7 us
    unnamed x1, local copies, waits for them, and re-layouts  1.3 us

profile of v3, /device:TPU:0, one launch (start us, length us, event | category | flops | bytes accessed | tf_op | source)
XLA Modules:
  0.0 28.0 jit_solution(7118462595817884518)
XLA Ops:
  0.0 26.7 %shard_map.46 = f32[8,256]{1,0:T(8,128)} custom-call(bf16[1,32,2048]{2,1,0:T(8,128)(2,1)} %test_hbm.1, bf16[1,2048,4096]{2,1,0:T(8,128)(2,1)} %inv_hbm.1, bf16[1,256,4096]{2,1,0:T(8,128)(2,1)} %train_hbm.1, f32[1,256]{1,0:T(1,128)} %weight_ref.1), custom_call_target="tpu_custom_call" | custom-call | tf_op jit(solution)/shard_map/pallas_call | solution.py:172
  26.7 1.3 %copy.6 = f32[8,256]{1,0:T(8,128)} copy(f32[8,256]{1,0:T(8,128)} %shard_map.46) | data formatting | bytes 16384
